TPU v7x, 32 devices: a whole 2x2x4 slice. The times are simulated.
32 devices in a mesh: row: 4 (over y, core), col: 8 (over z, x).
Axes of the slice: x: 2, y: 2, z: 4, core: 2. Of those that a mesh axis runs over, the one named last changes fastest.
Arguments:
- weight: bfloat16 [8192, 16384], P('row', 'col'), may hold values from -3 to 3
- momentum: float32 [8192, 16384], P('row', 'col'), may hold values from -100 to 100, as said below
- gradient: bfloat16 [8192, 16384], P('row', 'col'), may hold values from -6 to 6
- prev_basis: bfloat16 [16384, 512], P('col'), may hold values from -6 to 6
Outputs:
- new_weight: bfloat16 [8192, 16384], P('row', 'col')
- new_momentum: float32 [8192, 16384], P('row', 'col')
- new_basis: bfloat16 [16384, 512], P('col')
Inputs may be any that keep to these rules, and one draw needn't show every extreme that they name: momentum has rows and columns of different scales.
All inputs are finite; a program needn't handle non-finite values.
Results may differ from a plain program's by a relative error of at most 0.0021.
Values may be sent and summed in bfloat16 or wider, within the bound.
No kernel may reach another device: no remote copies, remote signals or barrier semaphores. Data moves between devices by JAX's collectives and lax.ppermute only.
A program may use at most 128 MiB of HBM per device.

v0:
```python
import jax
import jax.numpy as jnp
from jax import lax
from jax.sharding import PartitionSpec as P

M = 8192
N = 16384


decay_loss = 0.1
step_size = 0.4
epsilon = 1e-06


def orthogonalize(left_factor, gram_matrix):
    lower_tri = jnp.linalg.cholesky(gram_matrix)
    return jax.scipy.linalg.solve_triangular(lower_tri, left_factor.T, lower=True).T


def per_device(weight, momentum, gradient, prev_basis):
    high = lax.Precision.HIGHEST
    buffer = momentum + gradient.astype(jnp.float32)
    partial_left = jnp.dot(buffer, prev_basis.astype(jnp.float32), precision=high)
    left_factor = lax.psum(partial_left, "col")
    gram_matrix = lax.psum(jnp.dot(left_factor.T, left_factor, precision=high), "row")
    orthonormal = orthogonalize(left_factor, gram_matrix)
    right_piece = lax.psum_scatter(
        jnp.dot(buffer.T, orthonormal, precision=high), "row", scatter_dimension=0, tiled=True
    )
    square_sum = lax.psum(jnp.sum(right_piece * right_piece, axis=0), ("row", "col"))
    column_scale = jnp.sqrt(square_sum / N + epsilon)
    basis_piece = (right_piece / column_scale).astype(jnp.bfloat16)
    new_basis = lax.all_gather(basis_piece, "row", axis=0, tiled=True)
    basis_float = new_basis.astype(jnp.float32)
    new_momentum = buffer - decay_loss * jnp.dot(
        orthonormal * column_scale, basis_float.T, precision=high
    )
    update = jnp.dot(orthonormal, basis_float.T, precision=high)
    new_weight = (weight.astype(jnp.float32) - step_size * (M / N) ** 0.5 * update).astype(
        jnp.bfloat16
    )
    return (new_weight, new_momentum, new_basis)


def solution(mesh):
    return jax.shard_map(
        per_device,
        mesh=mesh,
        in_specs=(P("row", "col"), P("row", "col"), P("row", "col"), P("col", None)),
        out_specs=(P("row", "col"), P("row", "col"), P("col", None)),
        check_vma=False,
    )
```

profile of v0, /device:TPU:0, one launch (start us, length us, event | category | flops | bytes accessed | tf_op | source)
XLA Modules:
  0.0 632.8 jit_solution(8107940526218711960)
XLA Ops:
  7.2 0.0 all-reduce.4.cloned.1.call-start
  7.2 1.5 copy-done
  8.8 18.2 %fusion.1 = f32[2048,512]{1,0:T(8,128)} fusion(bf16[2048,512]{1,0:T(8,128)(2,1)S(1)} %copy-done, f32[2048,2048]{1,0:T(8,128)} %param.5, bf16[2048,2048]{1,0:T(8,128)(2,1)} %param.6), kind=kOutput, calls=%fused_computation.6 | convolution fusion | flops 25778192384 | bytes 31457280 | tf_op jit(solution)/shard_map/dot_general | solution.py:23
  26.9 0.0 all-reduce.4.cloned.1.call-update
  27.0 0.0 all-reduce.6.cloned.1.call-start
  27.0 159.2 %all-reduce.4.cloned.1.call-done = f32[2048,512]{1,0:T(8,128)} async-done(((f32[2048,512]{1,0:T(8,128)}), f32[2048,512]{1,0:T(8,128)}) %all-reduce.4.cloned.1.call-update) | async-done | bytes 4194320 | tf_op jit(solution)/shard_map/psum | solution.py:24
  186.2 11.4 %fusion.42 = f32[512,512]{0,1:T(8,128)} fusion(f32[2048,512]{1,0:T(8,128)} %all-reduce.4.cloned.1.call-done), kind=kOutput, calls=%fused_computation.81 | convolution fusion | flops 6442450944 | bytes 5242880 | tf_op jit(solution)/shard_map/dot_general | solution.py:25
  197.7 0.0 all-reduce.6.cloned.1.call-update
  197.7 0.2 reduce-scatter.2.cloned.1.call-start
  197.9 35.2 %all-reduce.6.cloned.1.call-done = f32[512,512]{0,1:T(8,128)} async-done(((f32[512,512]{0,1:T(8,128)}), f32[512,512]{0,1:T(8,128)}) %all-reduce.6.cloned.1.call-update) | async-done | bytes 1048592 | tf_op jit(solution)/shard_map/psum | solution.py:25
  233.1 1.6 copy.8
  234.7 1.4 fusion.18
  236.1 11.7 %cholesky.104 = f32[128,128]{1,0:T(8,128)S(1)} custom-call(f32[128,128]{1,0:T(8,128)S(1)} %cholesky.266), custom_call_target="Cholesky" | custom-call | tf_op jit(solution)/shard_map/jit(cholesky)/cholesky | solution.py:16
  247.9 9.8 %custom-call.31 = f32[1,128,128]{1,2,0:T(8,128)S(1)} custom-call(f32[1,128,128]{2,1,0:T(8,128)S(1)} %get-tuple-element.30), custom_call_target="InvertDiagBlocksLowerTriangular" | custom-call | tf_op jit(solution)/shard_map/jit(cholesky)/cholesky | solution.py:16
  257.7 0.1 cholesky.224
  257.8 0.3 constant_dynamic-update-slice_fusion.3
  258.1 0.3 convolution_subtract_fusion.2
  258.5 11.7 %cholesky.217 = f32[128,128]{1,0:T(8,128)S(1)} custom-call(f32[128,128]{1,0:T(8,128)S(1)} %cholesky.270), custom_call_target="Cholesky" | custom-call | tf_op jit(solution)/shard_map/jit(cholesky)/cholesky | solution.py:16
  270.2 10.2 %custom-call.32 = f32[1,128,128]{1,2,0:T(8,128)S(1)} custom-call(f32[1,128,128]{2,1,0:T(8,128)S(1)} %get-tuple-element.27), custom_call_target="InvertDiagBlocksLowerTriangular" | custom-call | tf_op jit(solution)/shard_map/jit(cholesky)/cholesky | solution.py:16
  280.4 0.3 convolution_dynamic-update-slice_fusion
  280.7 0.4 convolution_subtract_fusion.3
  281.1 11.7 %cholesky.238 = f32[128,128]{1,0:T(8,128)S(1)} custom-call(f32[128,128]{1,0:T(8,128)S(1)} %cholesky.275), custom_call_target="Cholesky" | custom-call | tf_op jit(solution)/shard_map/jit(cholesky)/cholesky | solution.py:16
  292.9 0.6 compare_reduce_fusion.1
  293.5 9.8 %custom-call.33 = f32[1,128,128]{1,2,0:T(8,128)S(1)} custom-call(f32[1,128,128]{2,1,0:T(8,128)S(1)} %get-tuple-element.24), custom_call_target="InvertDiagBlocksLowerTriangular" | custom-call | tf_op jit(solution)/shard_map/jit(cholesky)/cholesky | solution.py:16
  303.3 0.2 convolution_dynamic-update-slice_fusion.1
  303.5 0.4 convolution_subtract_fusion.4
  303.9 11.7 %cholesky.255 = f32[128,128]{1,0:T(8,128)S(1)} custom-call(f32[128,128]{1,0:T(8,128)S(1)} %convolution_subtract_fusion.4), custom_call_target="Cholesky" | custom-call | tf_op jit(solution)/shard_map/jit(cholesky)/cholesky | solution.py:16
  315.7 0.7 compare_reduce_fusion
  316.3 0.6 compare_reduce_fusion.2
  319.5 0.3 select_select_fusion
  319.8 8.0 %while.1 = (s32[]{:T(128)}, f32[512,512]{1,0:T(8,128)S(1)}, s32[4,2]{0,1:T(2,128)S(1)}, f32[4,128,128]{2,1,0:T(8,128)S(1)}, s32[]{:T(128)}) while((s32[]{:T(128)}, f32[512,512]{1,0:T(8,128)S(1)}, s32[4,2]{0,1:T(2,128)S(1)}, f32[4,128,128]{2,1,0:T(8,128)S(1)}, s32[]{:T(128)}) %tuple.31), condition=%wide.while_cond, body=%wide.while_body.sunk | while | flops 2 | bytes 131181 | solution.py:17
  319.8 0.1 constant_dynamic-slice_fusion.2
  319.9 0.5 fusion.54
  320.4 1.4 bitcast_dynamic-update-slice_fusion.2
  321.8 0.1 constant_dynamic-slice_fusion.2
  321.9 0.5 fusion.54
  322.4 1.4 bitcast_dynamic-update-slice_fusion.2
  323.8 0.1 constant_dynamic-slice_fusion.2
  323.9 0.5 fusion.54
  324.4 1.4 bitcast_dynamic-update-slice_fusion.2
  325.8 0.1 constant_dynamic-slice_fusion.2
  325.9 0.5 fusion.54
  326.4 1.4 bitcast_dynamic-update-slice_fusion.2
  327.9 39.3 %custom-call.34 = f32[4,128,128]{1,2,0:T(8,128)S(1)} custom-call(f32[4,128,128]{2,1,0:T(8,128)S(1)} %get-tuple-element.10), custom_call_target="InvertDiagBlocksLowerTriangular" | custom-call | tf_op jit(solution)/shard_map/jit(_solve_triangular)/triangular_solve | solution.py:17
  367.2 2.4 fusion.16
  369.6 3.1 convolution_subtract_fusion.1
  372.7 1.1 fusion.30
  373.8 5.0 convolution_subtract_fusion
  378.8 1.1 fusion.28
  379.9 7.2 %fusion.9 = f32[128,2048]{0,1:T(8,128)S(1)} fusion(f32[128,2048]{1,0:T(8,128)S(1)} %fusion.28, f32[128,2048]{1,0:T(8,128)S(1)} %fusion.30, f32[128,2048]{1,0:T(8,128)S(1)} %fusion.16, f32[512,2048]{0,1:T(8,128)S(1)} %bitcast.57, f32[512,512]{1,0:T(8,128)} %copy-done.7), kind=kOutput, calls=%fused_computation.15 | convolution fusion | flops 1209794560 | bytes 5439488 | tf_op jit(solution)/shard_map/jit(_solve_triangular)/triangular_solve | solution.py:17
  387.1 1.1 fusion.27
  388.2 1.0 copy-done.6
  389.2 56.3 %fusion = f32[2048,512]{1,0:T(8,128)} fusion(f32[2048,2048]{1,0:T(8,128)} %param.5, bf16[2048,2048]{1,0:T(8,128)(2,1)S(1)} %bitcast.59, f32[128,2048]{1,0:T(8,128)S(1)} %fusion.27, f32[128,2048]{1,0:T(8,128)S(1)} %fusion.28, f32[128,2048]{1,0:T(8,128)S(1)} %fusion.30, f32[128,2048]{1,0:T(8,128)S(1)} %fusion.16), kind=kOutput, calls=%fused_computation.5 | convolution fusion | flops 25781338112 | bytes 33554432 | tf_op jit(solution)/shard_map/dot_general | solution.py:28
  445.5 0.0 reduce-scatter.2.cloned.1.call-update
  445.6 0.0 all-gather.2.cloned.1.call-start
  445.6 45.2 %reduce-scatter.2.cloned.1.call-done = f32[512,512]{1,0:T(8,128)} async-done(((f32[2048,512]{1,0:T(8,128)}), f32[512,512]{1,0:T(8,128)}) %reduce-scatter.2.cloned.1.call-update) | async-done | bytes 1048592 | tf_op jit(solution)/shard_map/reduce_scatter | solution.py:27
  490.8 1.3 multiply_reduce_fusion
  492.1 39.3 %psum.23 = f32[512]{0:T(512)S(1)} all-reduce(f32[512]{0:T(512)S(1)} %multiply_reduce_fusion), channel_id=1, replica_groups=mesh['row'=4,'col'=8] {'row','col'}, use_global_device_ids=true, to_apply=%region_12.13 | all-reduce | flops 512 | bytes 4096 | tf_op jit(solution)/shard_map/psum | solution.py:30
  531.4 2.1 divide_convert_fusion
  533.5 0.0 all-gather.2.cloned.1.call-update
  533.6 23.5 %all-gather.2.cloned.1.call-done = bf16[2048,512]{1,0:T(8,128)(2,1)} async-done(((bf16[512,512]{1,0:T(8,128)(2,1)}), bf16[2048,512]{1,0:T(8,128)(2,1)}) %all-gather.2.cloned.1.call-update) | async-done | bytes 2097168 | tf_op jit(solution)/shard_map/all_gather | solution.py:33
  557.1 35.6 %multiply_subtract_fusion = f32[2048,2048]{1,0:T(8,128)} fusion(bf16[2048,512]{1,0:T(8,128)(2,1)} %all-gather.2.cloned.1.call-done, f32[2048,2048]{1,0:T(8,128)} %param.5, bf16[2048,2048]{1,0:T(8,128)(2,1)} %param.6, f32[512]{0:T(512)S(1)} %add_sqrt_fusion, f32[128,2048]{1,0:T(8,128)} %copy-done.6, f32[128,2048]{1,0:T(8,128)S(1)} %fusion.28, ...), kind=kOutput, calls=%fused_computation.2 | convolution fusion | flops 25790775296 | bytes 48236544 | tf_op jit(solution)/shard_map/dot_general | solution.py:35
  592.7 32.0 %subtract_convert_fusion = bf16[2048,2048]{1,0:T(8,128)(2,1)} fusion(bf16[2048,2048]{1,0:T(8,128)(2,1)} %param.4, bf16[2048,512]{1,0:T(8,128)(2,1)} %all-gather.2.cloned.1.call-done, f32[128,2048]{1,0:T(8,128)} %copy-done.6, f32[128,2048]{1,0:T(8,128)} %copy-done.4, f32[128,2048]{1,0:T(8,128)} %copy-done.3, f32[128,2048]{1,0:T(8,128)S(1)} %fusion.16), kind=kOutput, calls=%fused_computation.3 | convolution fusion | flops 25789726720 | bytes 23068672 | tf_op jit(solution)/shard_map/dot_general | solution.py:38
  624.7 1.3 copy.28
  (30 shorter events, 0.2 us)
Async XLA Ops:
  7.2 1.6 copy-start
  7.2 179.1 %all-reduce.4.cloned.1.call-start = ((), (), s32[]{:S(2)}) async-start(), calls=%async_computation.1 | async-start | bytes 8388608 | tf_op jit(solution)/shard_map/psum | solution.py:24
  27.0 206.1 %all-reduce.6.cloned.1.call-start = ((), (), s32[]{:S(2)}) async-start(), calls=%async_computation.2 | async-start | bytes 2097152 | tf_op jit(solution)/shard_map/psum | solution.py:25
  197.7 293.1 %reduce-scatter.2.cloned.1.call-start = ((), (), s32[]{:S(2)}) async-start(), calls=%async_computation.3 | async-start | bytes 5242880 | tf_op jit(solution)/shard_map/reduce_scatter | solution.py:27
  327.8 39.3 %copy-start.7 = (f32[512,512]{1,0:T(8,128)}, f32[512,512]{1,0:T(8,128)S(1)}, u32[]{:S(2)}) copy-start(f32[512,512]{1,0:T(8,128)S(1)} %get-tuple-element.99) | copy-start | bytes 3145732
  367.2 6.6 %copy-start.2 = (f32[2048,512]{1,0:T(8,128)S(1)}, f32[2048,512]{1,0:T(8,128)}, u32[]{:S(2)}) copy-start(f32[2048,512]{1,0:T(8,128)} %all-reduce.4.cloned.1.call-done) | copy-start | bytes 12582916
  372.7 16.5 %slice-start = ((s8[8388608]{0:T(1024)(128)(4,1)}), s8[4194304]{0:T(1024)(128)(4,1)S(1)}, s32[]{:S(2)}) async-start(s8[8388608]{0:T(1024)(128)(4,1)} %bitcast.58), calls=%async_computation.5 | async-start | bytes 8388608
  373.8 183.2 %copy-start.3 = (f32[128,2048]{1,0:T(8,128)}, f32[128,2048]{1,0:T(8,128)S(1)}, u32[]{:S(2)}) copy-start(f32[128,2048]{1,0:T(8,128)S(1)} %fusion.30) | copy-start | bytes 3145732
  378.8 10.4 %slice-start.1 = ((s8[8388608]{0:T(1024)(128)(4,1)}), s8[4194304]{0:T(1024)(128)(4,1)S(1)}, s32[]{:S(2)}) async-start(s8[8388608]{0:T(1024)(128)(4,1)} %bitcast.58), calls=%async_computation.6 | async-start | bytes 8388608
  379.9 177.2 %copy-start.4 = (f32[128,2048]{1,0:T(8,128)}, f32[128,2048]{1,0:T(8,128)S(1)}, u32[]{:S(2)}) copy-start(f32[128,2048]{1,0:T(8,128)S(1)} %fusion.28) | copy-start | bytes 3145732
  388.2 1.0 copy-start.6
  445.6 111.5 %all-gather.2.cloned.1.call-start = ((), (), s32[]{:S(2)}) async-start(), calls=%async_computation.4 | async-start | bytes 2621440 | tf_op jit(solution)/shard_map/all_gather | solution.py:33
  592.7 32.1 %copy-start.5 = (bf16[2048,512]{1,0:T(8,128)(2,1)S(1)}, bf16[2048,512]{1,0:T(8,128)(2,1)}, u32[]{:S(2)}) copy-start(bf16[2048,512]{1,0:T(8,128)(2,1)} %all-gather.2.cloned.1.call-done) | copy-start | bytes 6291460
  592.7 33.4 %copy-start.1 = (bf16[2048,512]{1,0:T(8,128)(2,1)S(1)}, bf16[2048,512]{1,0:T(8,128)(2,1)}, u32[]{:S(2)}) copy-start(bf16[2048,512]{1,0:T(8,128)(2,1)} %param.7) | copy-start | bytes 6291460
Sparse Core Ops, SparseCore 0:
  27.1 159.1 all-reduce.3
  197.8 35.2 all-reduce.5
  445.7 45.0 reduce-scatter.1
  533.7 23.3 all-gather.1
where the time goes:
time: 639 us; the launch traced here: 633 us
  waiting for transfers between devices  263 us (41%)
  matrix products  176 us (28%)
  other arithmetic  123 us (19%)
  blocking collectives  39.3 us (6%)
  between operations  16.8 us (3%)
  local copies, waits for them, and re-layouts  13.5 us (2%)
    psum x1, waiting for transfers between devices, per_device(): left_factor = lax.psum(partial_left, 'col')  159 us
    another operation x14, other arithmetic, orthogonalize(): lower_tri = jnp.linalg.cholesky(gram_matrix)  78.8 us
    dot_general x1, matrix products, per_device(): jnp.dot(buffer.T, orthonormal, precision=high)  56.3 us
    reduce_scatter x1, waiting for transfers between devices, per_device(): lax.psum_scatter(jnp.dot(buffer.T, orthonormal, precision=high), 'row', s...  45.2 us
    another operation x3, other arithmetic, orthogonalize(): jax.scipy.linalg.solve_triangular(lower_tri, left_factor.T, lower=True)  39.6 us
    psum x1, blocking collectives, per_device(): lax.psum(jnp.sum(right_piece * right_piece, axis=0), ('row', 'col'))  39.3 us
    dot_general x1, matrix products, per_device(): jnp.dot(orthonormal * column_scale, basis_float.T, precision=high)  35.6 us
    psum x1, waiting for transfers between devices, per_device(): lax.psum(jnp.dot(left_factor.T, left_factor, precision=high), 'row')  35.2 us
  transfers between devices with their start and end apart: 4, of which 4 were waited for; matrix products, arithmetic and copies ran while one was open for 0% of the time, Pallas kernels for 0%

commit v1 on v0

v1 whole, which is shorter than its diff:
```python
import functools
import jax
import jax.numpy as jnp
from jax import lax
from jax.experimental import pallas as pl
from jax.experimental.pallas import tpu as pltpu
from jax.sharding import PartitionSpec as P

HI = lax.Precision.HIGHEST
F32 = jnp.float32
NB = 128
G = 8


def factor_block(d, x):
    n = len(d)
    for b in range(n):
        own = d[b]
        cols = [jnp.broadcast_to(own[:, G * b + k : G * b + k + 1], (G, NB)) for k in range(G)]
        s = {}
        for i in range(G):
            for k in range(i + 1):
                s[i, k] = jnp.broadcast_to(cols[k][i : i + 1, :], (G, NB))
        inv = []
        low = {}
        for k in range(G):
            r = 1.0 / s[k, k]
            inv.append(r)
            for i in range(k + 1, G):
                low[i, k] = s[i, k] * r
            for i in range(k + 1, G):
                for j in range(k + 1, i + 1):
                    s[i, j] = s[i, j] - low[i, k] * s[j, k]
        rows = [
            [jnp.broadcast_to(m[k : k + 1, :], (G, NB)) for k in range(G)] for m in (own, x[b])
        ]
        for part in rows:
            for i in range(1, G):
                for k in range(i):
                    part[i] = part[i] - low[i, k] * part[k]
        sub = lax.broadcasted_iota(jnp.int32, (G, NB), 0)
        out = jnp.zeros((G, NB), F32)
        for k in range(G):
            out = jnp.where(sub == k, rows[1][k] * lax.rsqrt(s[k, k]), out)
        z = []
        for part in rows:
            t = [part[k] * inv[k] for k in range(G)]
            for k in range(G - 2, -1, -1):
                for i in range(k + 1, G):
                    t[k] = t[k] - low[i, k] * t[i]
            z.append(t)
        for g in range(b + 1, n):
            col = [jnp.broadcast_to(d[g][:, G * b + k : G * b + k + 1], (G, NB)) for k in range(G)]
            dd = [col[k] * z[0][k] for k in range(G)]
            xx = [col[k] * z[1][k] for k in range(G)]
            while len(dd) > 1:
                dd = [dd[i] + dd[i + 1] for i in range(0, len(dd), 2)]
                xx = [xx[i] + xx[i + 1] for i in range(0, len(xx), 2)]
            d[g] = d[g] - dd[0]
            x[g] = x[g] - xx[0]
        x[b] = out
    return x


def chol_kernel(g_ref, y_ref, a_ref, xb_ref):
    rank = g_ref.shape[0]
    nb = rank // NB
    a_ref[...] = g_ref[...]
    ri = lax.broadcasted_iota(jnp.int32, (rank, rank), 0)
    ci = lax.broadcasted_iota(jnp.int32, (rank, rank), 1)
    y_ref[...] = jnp.where(ri == ci, 1.0, 0.0).astype(F32)

    @pl.loop(0, nb)
    def _(p):
        at = pl.multiple_of(p * NB, NB)
        d = [a_ref[pl.ds(pl.multiple_of(at + G * i, G), G), pl.ds(at, NB)] for i in range(NB // G)]
        sub = lax.broadcasted_iota(jnp.int32, (G, NB), 0)
        lane = lax.broadcasted_iota(jnp.int32, (G, NB), 1)
        x = [jnp.where(lane == sub + G * i, 1.0, 0.0).astype(F32) for i in range(NB // G)]
        x = factor_block(d, x)
        for i in range(NB // G):
            xb_ref[pl.ds(G * i, G), :] = x[i]
        for q in range(nb):

            @pl.when(p == q)
            def _():
                s0, s1 = q * NB, (q + 1) * NB
                xb = xb_ref[...]
                if q:
                    y_ref[s0:s1, :s0] = jnp.dot(xb, y_ref[s0:s1, :s0], precision=HI)
                y_ref[s0:s1, s0:s1] = xb
                if q < nb - 1:
                    up = jnp.dot(xb, a_ref[s0:s1, s1:], precision=HI)
                    both = jnp.concatenate([up, y_ref[s0:s1, :s1]], axis=1)
                    upd = lax.dot_general(up, both, (((0,), (0,)), ((), ())), precision=HI)
                    w = rank - s1
                    a_ref[s1:, s1:] = a_ref[s1:, s1:] - upd[:, :w]
                    y_ref[s1:, :s1] = y_ref[s1:, :s1] - upd[:, w:]


def chol_inverse(g):
    rank = g.shape[0]
    return pl.pallas_call(
        chol_kernel,
        out_shape=jax.ShapeDtypeStruct((rank, rank), F32),
        scratch_shapes=[pltpu.VMEM((rank, rank), F32), pltpu.VMEM((NB, NB), F32)],
        name="chol",
    )(g)


BF16 = jnp.bfloat16
decay_loss = 0.1
step_size = 0.4
epsilon = 1e-06
CHUNKS = 4
TILE = 256
PARAMS = pltpu.CompilerParams(vmem_limit_bytes=56 * 2**20)


def halves(v):
    hi = v.astype(BF16)
    return hi, (v - hi.astype(F32)).astype(BF16)


def dot(a, b, dims=((1,), (0,))):
    return lax.dot_general(a, b, (dims, ((), ())), preferred_element_type=F32)


def dot3(a, b, dims=((1,), (0,))):
    ah, al = halves(a)
    bh, bl = halves(b)
    return dot(ah, bh, dims) + (dot(al, bh, dims) + dot(ah, bl, dims))


def left_kernel(m_ref, g_ref, q_ref, o_ref):
    hi, lo = halves(m_ref[...] + g_ref[...].astype(F32))
    o_ref[...] = dot(hi, q_ref[...]) + dot(lo, q_ref[...])


def left_chunk(momentum, gradient, basis, chunk):
    rows, cols = momentum.shape
    rank = basis.shape[1]
    steps = rows // CHUNKS // TILE
    tile = pl.BlockSpec((TILE, cols), lambda i: (chunk * steps + i, 0))
    return pl.pallas_call(
        left_kernel,
        grid=(steps,),
        in_specs=[tile, tile, pl.BlockSpec((cols, rank), lambda i: (0, 0))],
        out_specs=pl.BlockSpec((TILE, rank), lambda i: (i, 0)),
        out_shape=jax.ShapeDtypeStruct((rows // CHUNKS, rank), F32),
        compiler_params=PARAMS,
        name="left",
    )(momentum, gradient, basis)


def gram_kernel(l_ref, o_ref):
    @pl.when(pl.program_id(0) == 0)
    def _():
        o_ref[...] = jnp.zeros_like(o_ref)

    part = l_ref[...]
    o_ref[...] += lax.dot_general(part, part, (((0,), (0,)), ((), ())), precision=HI)


def gram(left):
    rows, rank = left.shape
    return pl.pallas_call(
        gram_kernel,
        grid=(rows // TILE,),
        in_specs=[pl.BlockSpec((TILE, rank), lambda i: (i, 0))],
        out_specs=pl.BlockSpec((rank, rank), lambda i: (0, 0)),
        out_shape=jax.ShapeDtypeStruct((rank, rank), F32),
        compiler_params=PARAMS,
        name="gram",
    )(left)


def back_kernel(m_ref, g_ref, l_ref, o_ref):
    @pl.when(pl.program_id(0) == 0)
    def _():
        o_ref[...] = jnp.zeros_like(o_ref)

    o_ref[...] += dot3(l_ref[...], m_ref[...] + g_ref[...].astype(F32), ((0,), (0,)))


def back(momentum, gradient, left):
    rows, cols = momentum.shape
    rank = left.shape[1]
    tile = pl.BlockSpec((TILE, cols), lambda i: (i, 0))
    return pl.pallas_call(
        back_kernel,
        grid=(rows // TILE,),
        in_specs=[tile, tile, pl.BlockSpec((TILE, rank), lambda i: (i, 0))],
        out_specs=pl.BlockSpec((rank, cols), lambda i: (0, 0)),
        out_shape=jax.ShapeDtypeStruct((rank, cols), F32),
        compiler_params=PARAMS,
        name="back",
    )(momentum, gradient, left)


def right_kernel(y_ref, w_ref, r_ref, s_ref):
    r = dot3(y_ref[...], w_ref[...])
    r_ref[...] = r
    total = jnp.sum(r * r, axis=1, keepdims=True)
    s_ref[...] = jnp.broadcast_to(total, s_ref.shape)


def right(inverse, back_sum):
    rank, cols = back_sum.shape
    return pl.pallas_call(
        right_kernel,
        out_shape=(
            jax.ShapeDtypeStruct((rank, cols), F32),
            jax.ShapeDtypeStruct((rank, 128), F32),
        ),
        compiler_params=PARAMS,
        name="right",
    )(inverse, back_sum)


def ortho_kernel(l_ref, y_ref, o_ref):
    o_ref[...] = dot3(l_ref[...], y_ref[...], ((1,), (1,)))


def ortho(left, inverse):
    rows, rank = left.shape
    tile = pl.BlockSpec((TILE, rank), lambda i: (i, 0))
    return pl.pallas_call(
        ortho_kernel,
        grid=(rows // TILE,),
        in_specs=[tile, pl.BlockSpec((rank, rank), lambda i: (0, 0))],
        out_specs=tile,
        out_shape=jax.ShapeDtypeStruct((rows, rank), F32),
        compiler_params=PARAMS,
        name="ortho",
    )(left, inverse)


def final_kernel(
    update_scale, w_ref, m_ref, g_ref, o_ref, r_ref, sc_ref, sr_ref, nw_ref, nm_ref, nb_ref, n_ref
):
    @pl.when(pl.program_id(0) == 0)
    def _():
        basis = r_ref[...] / sc_ref[...][:, :1]
        n_ref[...] = basis.astype(BF16)
        nb_ref[...] = basis.T.astype(BF16)

    basis = n_ref[...]
    ortho_part = o_ref[...]
    hi, lo = halves(ortho_part)
    scaled = (ortho_part * sr_ref[...][:1, :]).astype(BF16)
    nm_ref[...] = m_ref[...] + g_ref[...].astype(F32) - decay_loss * dot(scaled, basis)
    update = dot(hi, basis) + dot(lo, basis)
    nw_ref[...] = (w_ref[...].astype(F32) - update_scale * update).astype(BF16)


def final(update_scale, weight, momentum, gradient, orthonormal, right_t, scale):
    rows, cols = momentum.shape
    rank = orthonormal.shape[1]
    tile = pl.BlockSpec((TILE, cols), lambda i: (i, 0))
    whole = lambda a: pl.BlockSpec(a.shape, lambda i: (0, 0))
    row = jnp.broadcast_to(scale[:, 0][None, :], (8, rank))
    return pl.pallas_call(
        functools.partial(final_kernel, update_scale),
        grid=(rows // TILE,),
        in_specs=[
            tile,
            tile,
            tile,
            pl.BlockSpec((TILE, rank), lambda i: (i, 0)),
            whole(right_t),
            whole(scale),
            whole(row),
        ],
        out_specs=(tile, tile, pl.BlockSpec((cols, rank), lambda i: (0, 0))),
        out_shape=(
            jax.ShapeDtypeStruct((rows, cols), BF16),
            jax.ShapeDtypeStruct((rows, cols), F32),
            jax.ShapeDtypeStruct((cols, rank), BF16),
        ),
        scratch_shapes=[pltpu.VMEM((rank, cols), BF16)],
        compiler_params=PARAMS,
        name="final",
    )(weight, momentum, gradient, orthonormal, right_t, scale, row)


def swap(v, axis, size, bit):
    return lax.ppermute(v, axis, [(i, i ^ (1 << bit)) for i in range(size)])


def side(axis, bit):
    return (lax.axis_index(axis) >> bit) & 1


def halve(v, axis, size, bit):
    half = v.shape[0] // 2
    mine = side(axis, bit)
    send = lax.dynamic_slice_in_dim(v, (1 - mine) * half, half)
    keep = lax.dynamic_slice_in_dim(v, mine * half, half)
    return keep + swap(send, axis, size, bit)


def double(v, axis, size, bit):
    other = swap(v, axis, size, bit)
    half = v.shape[0]
    mine = side(axis, bit)
    out = jnp.zeros((2 * half,) + v.shape[1:], v.dtype)
    out = lax.dynamic_update_slice_in_dim(out, v, mine * half, 0)
    return lax.dynamic_update_slice_in_dim(out, other, (1 - mine) * half, 0)


def bits(size):
    return range(size.bit_length() - 1)


def per_device(mesh, weight, momentum, gradient, prev_basis):
    rows, cols = mesh.shape["row"], mesh.shape["col"]
    total_rows, total_cols = momentum.shape[0] * rows, momentum.shape[1] * cols
    pieces = []
    for chunk in range(CHUNKS):
        part = left_chunk(momentum, gradient, prev_basis, chunk)
        for bit in bits(cols):
            part = halve(part, "col", cols, bit)
        pieces.append(part)
    chunks = []
    for part in pieces:
        for bit in reversed(bits(cols)):
            part = double(part, "col", cols, bit)
        chunks.append(part)
    left = jnp.concatenate(chunks)

    gram_matrix = halve(gram(left), "row", rows, 0)
    back_sum = halve(back(momentum, gradient, left), "row", rows, 0)
    for bit in bits(rows)[1:]:
        gram_matrix = gram_matrix + swap(gram_matrix, "row", rows, bit)
        back_sum = back_sum + swap(back_sum, "row", rows, bit)
    gram_matrix = double(gram_matrix, "row", rows, 0)
    back_sum = double(back_sum, "row", rows, 0)

    inverse = chol_inverse(gram_matrix)
    right_t, square_sum = right(inverse, back_sum)
    for bit in bits(cols):
        square_sum = square_sum + swap(square_sum, "col", cols, bit)
    orthonormal = ortho(left, inverse)
    scale = jnp.sqrt(square_sum / total_cols + epsilon)
    update_scale = step_size * (total_rows / total_cols) ** 0.5
    return final(update_scale, weight, momentum, gradient, orthonormal, right_t, scale)


def solution(mesh):
    return jax.shard_map(
        functools.partial(per_device, mesh),
        mesh=mesh,
        in_specs=(P("row", "col"), P("row", "col"), P("row", "col"), P("col", None)),
        out_specs=(P("row", "col"), P("row", "col"), P("col", None)),
        check_vma=False,
    )
```

time: 639 us -> 357 us (0.56)
  matrix products: 176 us -> 0 us
  Pallas kernels: 0 us -> 125 us
  other arithmetic: 123 us -> 13 us
  waiting for transfers between devices: 263 us -> 164 us
  blocking collectives: 39.3 us -> 0 us
  starting transfers between devices: 0.34 us -> 33.2 us
  between operations: 16.8 us -> 1.17 us
    psum x2 -> x0, waiting for transfers between devices: 194 us -> none  [the longest x1 159 us: per_device(): left_factor = lax.psum(partial_left, 'col')]
    ppermute x0 -> x33, waiting for transfers between devices: none -> 164 us  [swap(): return lax.ppermute(v, axis, [(i, i ^ 1 << bit) for i in range(size)])]
    dot_general x5 -> x0, matrix products: 154 us -> none  [the longest x1 56.3 us: per_device(): jnp.dot(buffer.T, orthonormal, precision=high)]
    pallas_call x0 -> x10, Pallas kernels: none -> 125 us  [the longest x1 27.1 us: chol_inverse(): pl.pallas_call(chol_kernel, out_shape=jax.ShapeDtypeStruct((rank, rank),...]
    another operation x17 -> x0, other arithmetic: 118 us -> none  [the longest x14 78.8 us: orthogonalize(): lower_tri = jnp.linalg.cholesky(gram_matrix)]
    reduce_scatter x1 -> x0, waiting for transfers between devices: 45.2 us -> none  [per_device(): lax.psum_scatter(jnp.dot(buffer.T, orthonormal, precision=high), 'row', s...]
    psum x1 -> x0, blocking collectives: 39.3 us -> none  [per_device(): lax.psum(jnp.sum(right_piece * right_piece, axis=0), ('row', 'col'))]
    ppermute x0 -> x33, starting transfers between devices: none -> 33.2 us  [swap(): return lax.ppermute(v, axis, [(i, i ^ 1 << bit) for i in range(size)])]
  transfers between devices with their start and end apart: 4 -> 33, of which waited for: 4 -> 23; matrix products, arithmetic and copies ran while one was open for 0% -> 5% of each run, Pallas kernels for 0% -> 18%
where the time goes in v1:
time: 357 us; the launch traced here: 356 us
  waiting for transfers between devices  164 us (46%)
  Pallas kernels  125 us (35%)
  starting transfers between devices  33.2 us (9%)
  local copies, waits for them, and re-layouts  19.3 us (5%)
  other arithmetic  13 us (4%)
    ppermute x33, waiting for transfers between devices, swap(): return lax.ppermute(v, axis, [(i, i ^ 1 << bit) for i in range(size)])  164 us
    ppermute x33, starting transfers between devices, swap(): return lax.ppermute(v, axis, [(i, i ^ 1 << bit) for i in range(size)])  33.2 us
    pallas_call x1, Pallas kernels, chol_inverse(): pl.pallas_call(chol_kernel, out_shape=jax.ShapeDtypeStruct((rank, rank),...  27.1 us
    pallas_call x1, Pallas kernels, final(): pl.pallas_call(functools.partial(final_kernel, update_scale), grid=(rows...  26.8 us
    pallas_call x4, Pallas kernels, left_chunk(): pl.pallas_call(left_kernel, grid=(steps,), in_specs=[tile, tile, pl.Block...  23.6 us
    pallas_call x1, Pallas kernels, back(): pl.pallas_call(back_kernel, grid=(rows // TILE,), in_specs=[tile, tile, p...  19.8 us
    dynamic_slice x14, local copies, waits for them, and re-layouts, halve(): send = lax.dynamic_slice_in_dim(v, (1 - mine) * half, half)  12.1 us
    pallas_call x1, Pallas kernels, gram(): pl.pallas_call(gram_kernel, grid=(rows // TILE,), in_specs=[pl.BlockSpec(...  10.5 us
  transfers between devices with their start and end apart: 33, of which 23 were waited for; matrix products, arithmetic and copies ran while one was open for 5% of the time, Pallas kernels for 18%

profile of v1, /device:TPU:0, one launch (start us, length us, event | category | flops | bytes accessed | tf_op | source)
XLA Modules:
  0.0 355.7 jit_solution(9408200016737527157)
XLA Ops:
  0.6 5.9 %left.5 = f32[512,512]{1,0:T(8,128)} custom-call(f32[2048,2048]{1,0:T(8,128)} %m_ref.11, bf16[2048,2048]{1,0:T(8,128)(2,1)} %g_ref.11, bf16[2048,512]{1,0:T(8,128)(2,1)} %q_ref.7), custom_call_target="tpu_custom_call" | custom-call | tf_op jit(solution)/shard_map/left/pallas_call | solution.py:145
  6.6 1.9 constant_dynamic-slice_fusion.10
  8.4 3.0 collective-permute-start.6
  11.4 5.9 %left.4 = f32[512,512]{1,0:T(8,128)} custom-call(f32[2048,2048]{1,0:T(8,128)} %m_ref.11, bf16[2048,2048]{1,0:T(8,128)(2,1)} %g_ref.11, bf16[2048,512]{1,0:T(8,128)(2,1)} %q_ref.7), custom_call_target="tpu_custom_call" | custom-call | tf_op jit(solution)/shard_map/left/pallas_call | solution.py:145
  17.3 1.9 constant_dynamic-slice_fusion.13
  19.2 5.9 %left.7 = f32[512,512]{1,0:T(8,128)} custom-call(f32[2048,2048]{1,0:T(8,128)} %m_ref.11, bf16[2048,2048]{1,0:T(8,128)(2,1)} %g_ref.11, bf16[2048,512]{1,0:T(8,128)(2,1)} %q_ref.7), custom_call_target="tpu_custom_call" | custom-call | tf_op jit(solution)/shard_map/left/pallas_call | solution.py:145
  25.1 1.9 constant_dynamic-slice_fusion.4
  27.0 2.0 collective-permute-start.18
  29.0 5.9 %left.6 = f32[512,512]{1,0:T(8,128)} custom-call(f32[2048,2048]{1,0:T(8,128)} %m_ref.11, bf16[2048,2048]{1,0:T(8,128)(2,1)} %g_ref.11, bf16[2048,512]{1,0:T(8,128)(2,1)} %q_ref.7), custom_call_target="tpu_custom_call" | custom-call | tf_op jit(solution)/shard_map/left/pallas_call | solution.py:145
  34.9 2.0 constant_dynamic-slice_fusion.7
  37.0 1.3 dynamic-slice_add_fusion.4
  38.3 2.1 collective-permute-start.7
  40.4 1.1 dynamic-slice_add_fusion.5
  41.6 5.3 %collective-permute-done.18 = f32[256,512]{1,0:T(8,128)} collective-permute-done((f32[256,512]{1,0:T(8,128)}, f32[256,512]{1,0:T(8,128)}, u32[]{:S(2)}, u32[]{:S(2)}) %collective-permute-start.18) | collective-permute-done | bytes 524320 | tf_op jit(solution)/shard_map/ppermute | solution.py:288
  47.0 1.1 dynamic-slice_add_fusion.2
  48.1 2.2 collective-permute-start.19
  50.3 7.1 %collective-permute-done.12 = f32[256,512]{1,0:T(8,128)} collective-permute-done((f32[256,512]{1,0:T(8,128)}, f32[256,512]{1,0:T(8,128)}, u32[]{:S(2)}, u32[]{:S(2)}) %collective-permute-start.12) | collective-permute-done | bytes 524320 | tf_op jit(solution)/shard_map/ppermute | solution.py:288
  57.3 1.1 dynamic-slice_add_fusion.3
  58.5 1.9 collective-permute-start.13
  60.5 2.7 collective-permute-start.8
  63.7 2.7 collective-permute-start.20
  66.3 4.2 %collective-permute-done.13 = f32[128,512]{1,0:T(8,128)S(1)} collective-permute-done((f32[128,512]{1,0:T(8,128)S(1)}, f32[128,512]{1,0:T(8,128)S(1)}, u32[]{:S(2)}, u32[]{:S(2)}) %collective-permute-start.13) | collective-permute-done | bytes 262176 | tf_op jit(solution)/shard_map/ppermute | solution.py:288
  70.6 1.5 collective-permute-start.14
  72.1 1.6 collective-permute-start.9
  73.7 10.8 %collective-permute-done.2 = f32[64,512]{1,0:T(8,128)S(1)} collective-permute-done((f32[64,512]{1,0:T(8,128)S(1)}, f32[64,512]{1,0:T(8,128)S(1)}, u32[]{:S(2)}, u32[]{:S(2)}) %collective-permute-start.2) | collective-permute-done | bytes 131104 | tf_op jit(solution)/shard_map/ppermute | solution.py:288
  84.7 2.7 collective-permute-done.20
  87.7 8.1 %collective-permute-done.14 = f32[64,512]{1,0:T(8,128)S(1)} collective-permute-done((f32[64,512]{1,0:T(8,128)S(1)}, f32[64,512]{1,0:T(8,128)S(1)}, u32[]{:S(2)}, u32[]{:S(2)}) %collective-permute-start.14) | collective-permute-done | bytes 131104 | tf_op jit(solution)/shard_map/ppermute | solution.py:288
  95.9 4.2 %collective-permute-done.9 = f32[64,512]{1,0:T(8,128)S(1)} collective-permute-done((f32[64,512]{1,0:T(8,128)S(1)}, f32[64,512]{1,0:T(8,128)S(1)}, u32[]{:S(2)}, u32[]{:S(2)}) %collective-permute-start.9) | collective-permute-done | bytes 131104 | tf_op jit(solution)/shard_map/ppermute | solution.py:288
  100.8 3.6 %collective-permute-done.3 = f32[64,512]{1,0:T(8,128)S(1)} collective-permute-done((f32[64,512]{1,0:T(8,128)S(1)}, f32[64,512]{1,0:T(8,128)S(1)}, u32[]{:S(2)}, u32[]{:S(2)}) %collective-permute-start.3) | collective-permute-done | bytes 131104 | tf_op jit(solution)/shard_map/ppermute | solution.py:288
  104.5 2.6 collective-permute-done.21
  107.3 1.4 collective-permute-done.15
  109.5 4.8 %collective-permute-done.10 = f32[128,512]{1,0:T(8,128)S(1)} collective-permute-done((f32[128,512]{1,0:T(8,128)S(1)}, f32[128,512]{1,0:T(8,128)S(1)}, u32[]{:S(2)}, u32[]{:S(2)}) %collective-permute-start.10) | collective-permute-done | bytes 262176 | tf_op jit(solution)/shard_map/ppermute | solution.py:288
  114.4 1.5 collective-permute-start.11
  115.8 4.1 %collective-permute-done.4 = f32[128,512]{1,0:T(8,128)S(1)} collective-permute-done((f32[128,512]{1,0:T(8,128)S(1)}, f32[128,512]{1,0:T(8,128)S(1)}, u32[]{:S(2)}, u32[]{:S(2)}) %collective-permute-start.4) | collective-permute-done | bytes 262176 | tf_op jit(solution)/shard_map/ppermute | solution.py:288
  120.0 1.5 collective-permute-start.5
  121.4 4.1 %collective-permute-done.22 = f32[128,512]{1,0:T(8,128)S(1)} collective-permute-done((f32[128,512]{1,0:T(8,128)S(1)}, f32[128,512]{1,0:T(8,128)S(1)}, u32[]{:S(2)}, u32[]{:S(2)}) %collective-permute-start.22) | collective-permute-done | bytes 262176 | tf_op jit(solution)/shard_map/ppermute | solution.py:288
  125.6 1.5 collective-permute-start.23
  127.0 2.5 collective-permute-done.16
  129.6 1.6 collective-permute-start.17
  131.9 8.6 %collective-permute-done.5 = f32[256,512]{1,0:T(8,128)S(1)} collective-permute-done((f32[256,512]{1,0:T(8,128)S(1)}, f32[256,512]{1,0:T(8,128)S(1)}, u32[]{:S(2)}, u32[]{:S(2)}) %collective-permute-start.5) | collective-permute-done | bytes 524320 | tf_op jit(solution)/shard_map/ppermute | solution.py:288
  140.6 18.3 %collective-permute-done.17 = f32[256,512]{1,0:T(8,128)S(1)} collective-permute-done((f32[256,512]{1,0:T(8,128)S(1)}, f32[256,512]{1,0:T(8,128)S(1)}, u32[]{:S(2)}, u32[]{:S(2)}) %collective-permute-start.17) | collective-permute-done | bytes 524320 | tf_op jit(solution)/shard_map/ppermute | solution.py:288
  159.0 2.5 pad_maximum_fusion.l_ref
  161.5 19.8 %back.1 = f32[512,2048]{1,0:T(8,128)} custom-call(f32[2048,2048]{1,0:T(8,128)} %m_ref.11, bf16[2048,2048]{1,0:T(8,128)(2,1)} %g_ref.11, f32[2048,512]{1,0:T(8,128)} %pad_maximum_fusion.l_ref), custom_call_target="tpu_custom_call" | custom-call | tf_op jit(solution)/shard_map/back/pallas_call | solution.py:190
  181.3 3.1 constant_dynamic-slice_fusion
  184.4 4.4 %collective-permute-done.27 = f32[256,2048]{1,0:T(8,128)S(1)} collective-permute-done((f32[256,2048]{1,0:T(8,128)}, f32[256,2048]{1,0:T(8,128)S(1)}, u32[]{:S(2)}, u32[]{:S(2)}) %collective-permute-start.27) | collective-permute-done | bytes 2097184 | tf_op jit(solution)/shard_map/ppermute | solution.py:288
  188.8 1.8 dynamic-slice_add_fusion
  190.6 1.6 collective-permute-start.28
  192.2 10.5 %gram.1 = f32[512,512]{1,0:T(8,128)} custom-call(f32[2048,512]{1,0:T(8,128)} %pad_maximum_fusion.l_ref), custom_call_target="tpu_custom_call" | custom-call | tf_op jit(solution)/shard_map/gram/pallas_call | solution.py:167
  202.7 1.1 constant_dynamic-slice_fusion.1
  203.9 34.5 %collective-permute-done.28 = f32[256,2048]{1,0:T(8,128)S(1)} collective-permute-done((f32[256,2048]{1,0:T(8,128)S(1)}, f32[256,2048]{1,0:T(8,128)S(1)}, u32[]{:S(2)}, u32[]{:S(2)}) %collective-permute-start.28) | collective-permute-done | bytes 2097184 | tf_op jit(solution)/shard_map/ppermute | solution.py:288
  238.3 2.5 broadcast_in_dim.10
  240.9 2.5 constant_dynamic-update-slice_fusion.1
  243.5 1.6 collective-permute-start.25
  245.1 12.8 %collective-permute-done.25 = f32[256,512]{1,0:T(8,128)S(1)} collective-permute-done((f32[256,512]{1,0:T(8,128)S(1)}, f32[256,512]{1,0:T(8,128)S(1)}, u32[]{:S(2)}, u32[]{:S(2)}) %collective-permute-start.25) | collective-permute-done | bytes 524320 | tf_op jit(solution)/shard_map/ppermute | solution.py:288
  258.2 1.9 collective-permute-done.26
  261.2 27.1 %chol.1.y_ref = f32[512,512]{1,0:T(8,128)} custom-call(f32[512,512]{1,0:T(8,128)} %copy-done.4), custom_call_target="tpu_custom_call" | custom-call | tf_op jit(solution)/shard_map/chol/pallas_call | solution.py:103
  288.3 1.5 constant_dynamic-update-slice_fusion.w_ref
  289.7 8.1 %right.1 = (f32[512,2048]{1,0:T(8,128)}, f32[512,128]{1,0:T(8,128)}) custom-call(f32[512,512]{1,0:T(8,128)} %chol.1.y_ref, f32[512,2048]{1,0:T(8,128)} %constant_dynamic-update-slice_fusion.w_ref), custom_call_target="tpu_custom_call" | custom-call | tf_op jit(solution)/shard_map/right/pallas_call | solution.py:210
  297.8 1.6 collective-permute-start.30
  299.4 7.0 %collective-permute-done.30 = f32[512,128]{1,0:T(8,128)S(1)} collective-permute-done((f32[512,128]{1,0:T(8,128)}, f32[512,128]{1,0:T(8,128)S(1)}, u32[]{:S(2)}, u32[]{:S(2)}) %collective-permute-start.30) | collective-permute-done | bytes 262176 | tf_op jit(solution)/shard_map/ppermute | solution.py:288
  307.4 7.5 %collective-permute-done.31 = f32[512,128]{1,0:T(8,128)S(1)} collective-permute-done((f32[512,128]{1,0:T(8,128)S(1)}, f32[512,128]{1,0:T(8,128)S(1)}, u32[]{:S(2)}, u32[]{:S(2)}) %collective-permute-start.31) | collective-permute-done | bytes 262176 | tf_op jit(solution)/shard_map/ppermute | solution.py:288
  315.2 9.1 %ortho.1.o_ref = f32[2048,512]{1,0:T(8,128)} custom-call(f32[2048,512]{1,0:T(8,128)} %pad_maximum_fusion.l_ref, f32[512,512]{1,0:T(8,128)} %chol.1.y_ref), custom_call_target="tpu_custom_call" | custom-call | tf_op jit(solution)/shard_map/ortho/pallas_call | solution.py:228
  324.3 3.8 %collective-permute-done.32 = f32[512,128]{1,0:T(8,128)S(1)} collective-permute-done((f32[512,128]{1,0:T(8,128)S(1)}, f32[512,128]{1,0:T(8,128)S(1)}, u32[]{:S(2)}, u32[]{:S(2)}) %collective-permute-start.32) | collective-permute-done | bytes 262176 | tf_op jit(solution)/shard_map/ppermute | solution.py:288
  329.0 26.8 %final.1 = (bf16[2048,2048]{1,0:T(8,128)(2,1)}, f32[2048,2048]{1,0:T(8,128)}, bf16[2048,512]{1,0:T(8,128)(2,1)}) custom-call(bf16[2048,2048]{1,0:T(8,128)(2,1)} %w_ref.1, f32[2048,2048]{1,0:T(8,128)} %m_ref.11, bf16[2048,2048]{1,0:T(8,128)(2,1)} %g_ref.11, f32[2048,512]{1,0:T(8,128)} %ortho.1.o_ref, f32[512,2048]{1,0:T(8,128)} %get-tuple-element.5.r_ref, ...), custom_call_target="tpu_custom_call" | custom-call | tf_op jit(solution)/shard_map/final/pallas_call | solution.py:263
  (96 shorter events, 8.0 us)
Async XLA Ops:
  8.4 28.6 %collective-permute-start.6 = (f32[256,512]{1,0:T(8,128)}, f32[256,512]{1,0:T(8,128)}, u32[]{:S(2)}, u32[]{:S(2)}) collective-permute-start(f32[256,512]{1,0:T(8,128)} %constant_dynamic-slice_fusion.10), channel_id=1, source_target_pairs={{0,1},{1,0},{2,3},{3,2},{4,5},{5,4},{6,7},{7,6},{8,9},{9,8},{10,11... | collective-permute-start | bytes 1572872 | tf_op jit(solution)/shard_map/ppermute | solution.py:288
  19.2 21.2 %collective-permute-start = (f32[256,512]{1,0:T(8,128)}, f32[256,512]{1,0:T(8,128)}, u32[]{:S(2)}, u32[]{:S(2)}) collective-permute-start(f32[256,512]{1,0:T(8,128)} %constant_dynamic-slice_fusion.13), channel_id=1, source_target_pairs={{0,1},{1,0},{2,3},{3,2},{4,5},{5,4},{6,7},{7,6},{8,9},{9,8},{10,11... | collective-permute-start | bytes 1572872 | tf_op jit(solution)/shard_map/ppermute | solution.py:288
  27.0 13.4 %copy-start.2 = (f32[512,512]{1,0:T(8,128)S(1)}, f32[512,512]{1,0:T(8,128)}, u32[]{:S(2)}) copy-start(f32[512,512]{1,0:T(8,128)} %left.4) | copy-start | bytes 3145732
  27.0 20.0 %collective-permute-start.18 = (f32[256,512]{1,0:T(8,128)}, f32[256,512]{1,0:T(8,128)}, u32[]{:S(2)}, u32[]{:S(2)}) collective-permute-start(f32[256,512]{1,0:T(8,128)} %constant_dynamic-slice_fusion.4), channel_id=1, source_target_pairs={{0,1},{1,0},{2,3},{3,2},{4,5},{5,4},{6,7},{7,6},{8,9},{9,8},{10,11... | collective-permute-start | bytes 1572872 | tf_op jit(solution)/shard_map/ppermute | solution.py:288
  34.9 12.1 %copy-start.1 = (f32[512,512]{1,0:T(8,128)S(1)}, f32[512,512]{1,0:T(8,128)}, u32[]{:S(2)}) copy-start(f32[512,512]{1,0:T(8,128)} %left.7) | copy-start | bytes 3145732
  34.9 22.5 %copy-start = (f32[512,512]{1,0:T(8,128)S(1)}, f32[512,512]{1,0:T(8,128)}, u32[]{:S(2)}) copy-start(f32[512,512]{1,0:T(8,128)} %left.6) | copy-start | bytes 3145732
  36.9 20.4 %collective-permute-start.12 = (f32[256,512]{1,0:T(8,128)}, f32[256,512]{1,0:T(8,128)}, u32[]{:S(2)}, u32[]{:S(2)}) collective-permute-start(f32[256,512]{1,0:T(8,128)} %constant_dynamic-slice_fusion.7), channel_id=1, source_target_pairs={{0,1},{1,0},{2,3},{3,2},{4,5},{5,4},{6,7},{7,6},{8,9},{9,8},{10,11... | collective-permute-start | bytes 1572872 | tf_op jit(solution)/shard_map/ppermute | solution.py:288
  38.3 22.1 %collective-permute-start.7 = (f32[128,512]{1,0:T(8,128)S(1)}, f32[128,512]{1,0:T(8,128)S(1)}, u32[]{:S(2)}, u32[]{:S(2)}) collective-permute-start(f32[128,512]{1,0:T(8,128)S(1)} %constant_dynamic-slice_fusion.9), channel_id=1, source_target_pairs={{0,2},{1,3},{2,0},{3,1},{4,6},{5,7},{6,4},{7,5},{8,10},{9,11},{10,... | collective-permute-start | bytes 786440 | tf_op jit(solution)/shard_map/ppermute | solution.py:288
  41.6 21.6 %collective-permute-start.1 = (f32[128,512]{1,0:T(8,128)S(1)}, f32[128,512]{1,0:T(8,128)S(1)}, u32[]{:S(2)}, u32[]{:S(2)}) collective-permute-start(f32[128,512]{1,0:T(8,128)S(1)} %constant_dynamic-slice_fusion.12), channel_id=1, source_target_pairs={{0,2},{1,3},{2,0},{3,1},{4,6},{5,7},{6,4},{7,5},{8,10},{9,11},{10,... | collective-permute-start | bytes 786440 | tf_op jit(solution)/shard_map/ppermute | solution.py:288
  48.1 15.5 %collective-permute-start.19 = (f32[128,512]{1,0:T(8,128)S(1)}, f32[128,512]{1,0:T(8,128)S(1)}, u32[]{:S(2)}, u32[]{:S(2)}) collective-permute-start(f32[128,512]{1,0:T(8,128)S(1)} %constant_dynamic-slice_fusion.3), channel_id=1, source_target_pairs={{0,2},{1,3},{2,0},{3,1},{4,6},{5,7},{6,4},{7,5},{8,10},{9,11},{10,... | collective-permute-start | bytes 786440 | tf_op jit(solution)/shard_map/ppermute | solution.py:288
  58.5 12.0 %collective-permute-start.13 = (f32[128,512]{1,0:T(8,128)S(1)}, f32[128,512]{1,0:T(8,128)S(1)}, u32[]{:S(2)}, u32[]{:S(2)}) collective-permute-start(f32[128,512]{1,0:T(8,128)S(1)} %constant_dynamic-slice_fusion.6), channel_id=1, source_target_pairs={{0,2},{1,3},{2,0},{3,1},{4,6},{5,7},{6,4},{7,5},{8,10},{9,11},{10,... | collective-permute-start | bytes 786440 | tf_op jit(solution)/shard_map/ppermute | solution.py:288
  60.5 11.6 %collective-permute-start.8 = (f32[64,512]{1,0:T(8,128)S(1)}, f32[64,512]{1,0:T(8,128)S(1)}, u32[]{:S(2)}, u32[]{:S(2)}) collective-permute-start(f32[64,512]{1,0:T(8,128)S(1)} %constant_dynamic-slice_fusion.8), channel_id=1, source_target_pairs={{0,4},{1,5},{2,6},{3,7},{4,0},{5,1},{6,2},{7,3},{8,12},{9,13},{10,... | collective-permute-start | bytes 393224 | tf_op jit(solution)/shard_map/ppermute | solution.py:288
  63.2 21.3 %collective-permute-start.2 = (f32[64,512]{1,0:T(8,128)S(1)}, f32[64,512]{1,0:T(8,128)S(1)}, u32[]{:S(2)}, u32[]{:S(2)}) collective-permute-start(f32[64,512]{1,0:T(8,128)S(1)} %constant_dynamic-slice_fusion.11), channel_id=1, source_target_pairs={{0,4},{1,5},{2,6},{3,7},{4,0},{5,1},{6,2},{7,3},{8,12},{9,13},{10,... | collective-permute-start | bytes 393224 | tf_op jit(solution)/shard_map/ppermute | solution.py:288
  63.7 23.7 %collective-permute-start.20 = (f32[64,512]{1,0:T(8,128)S(1)}, f32[64,512]{1,0:T(8,128)S(1)}, u32[]{:S(2)}, u32[]{:S(2)}) collective-permute-start(f32[64,512]{1,0:T(8,128)S(1)} %constant_dynamic-slice_fusion.2), channel_id=1, source_target_pairs={{0,4},{1,5},{2,6},{3,7},{4,0},{5,1},{6,2},{7,3},{8,12},{9,13},{10,... | collective-permute-start | bytes 393224 | tf_op jit(solution)/shard_map/ppermute | solution.py:288
  70.6 25.2 %collective-permute-start.14 = (f32[64,512]{1,0:T(8,128)S(1)}, f32[64,512]{1,0:T(8,128)S(1)}, u32[]{:S(2)}, u32[]{:S(2)}) collective-permute-start(f32[64,512]{1,0:T(8,128)S(1)} %constant_dynamic-slice_fusion.5), channel_id=1, source_target_pairs={{0,4},{1,5},{2,6},{3,7},{4,0},{5,1},{6,2},{7,3},{8,12},{9,13},{10,... | collective-permute-start | bytes 393224 | tf_op jit(solution)/shard_map/ppermute | solution.py:288
  72.1 27.9 %collective-permute-start.9 = (f32[64,512]{1,0:T(8,128)S(1)}, f32[64,512]{1,0:T(8,128)S(1)}, u32[]{:S(2)}, u32[]{:S(2)}) collective-permute-start(f32[64,512]{1,0:T(8,128)S(1)} %get-tuple-element.14), channel_id=1, source_target_pairs={{0,4},{1,5},{2,6},{3,7},{4,0},{5,1},{6,2},{7,3},{8,12},{9,13},{10,... | collective-permute-start | bytes 393224 | tf_op jit(solution)/shard_map/ppermute | solution.py:288
  84.6 19.7 %collective-permute-start.3 = (f32[64,512]{1,0:T(8,128)S(1)}, f32[64,512]{1,0:T(8,128)S(1)}, u32[]{:S(2)}, u32[]{:S(2)}) collective-permute-start(f32[64,512]{1,0:T(8,128)S(1)} %get-tuple-element.12), channel_id=1, source_target_pairs={{0,4},{1,5},{2,6},{3,7},{4,0},{5,1},{6,2},{7,3},{8,12},{9,13},{10,... | collective-permute-start | bytes 393224 | tf_op jit(solution)/shard_map/ppermute | solution.py:288
  87.4 19.7 %collective-permute-start.21 = (f32[64,512]{1,0:T(8,128)S(1)}, f32[64,512]{1,0:T(8,128)S(1)}, u32[]{:S(2)}, u32[]{:S(2)}) collective-permute-start(f32[64,512]{1,0:T(8,128)S(1)} %get-tuple-element.18), channel_id=1, source_target_pairs={{0,4},{1,5},{2,6},{3,7},{4,0},{5,1},{6,2},{7,3},{8,12},{9,13},{10,... | collective-permute-start | bytes 393224 | tf_op jit(solution)/shard_map/ppermute | solution.py:288
  95.8 12.9 %collective-permute-start.15 = (f32[64,512]{1,0:T(8,128)S(1)}, f32[64,512]{1,0:T(8,128)S(1)}, u32[]{:S(2)}, u32[]{:S(2)}) collective-permute-start(f32[64,512]{1,0:T(8,128)S(1)} %get-tuple-element.16), channel_id=1, source_target_pairs={{0,4},{1,5},{2,6},{3,7},{4,0},{5,1},{6,2},{7,3},{8,12},{9,13},{10,... | collective-permute-start | bytes 393224 | tf_op jit(solution)/shard_map/ppermute | solution.py:288
  100.1 14.2 %collective-permute-start.10 = (f32[128,512]{1,0:T(8,128)S(1)}, f32[128,512]{1,0:T(8,128)S(1)}, u32[]{:S(2)}, u32[]{:S(2)}) collective-permute-start(f32[128,512]{1,0:T(8,128)S(1)} %constant_dynamic-update-slice_fusion.20), channel_id=1, source_target_pairs={{0,2},{1,3},{2,0},{3,1},{4,6},{5,7},{6,4},{7,5},{8,10},{9,11},{10,... | collective-permute-start | bytes 786440 | tf_op jit(solution)/shard_map/ppermute | solution.py:288
  104.3 15.6 %collective-permute-start.4 = (f32[128,512]{1,0:T(8,128)S(1)}, f32[128,512]{1,0:T(8,128)S(1)}, u32[]{:S(2)}, u32[]{:S(2)}) collective-permute-start(f32[128,512]{1,0:T(8,128)S(1)} %constant_dynamic-update-slice_fusion.26), channel_id=1, source_target_pairs={{0,2},{1,3},{2,0},{3,1},{4,6},{5,7},{6,4},{7,5},{8,10},{9,11},{10,... | collective-permute-start | bytes 786440 | tf_op jit(solution)/shard_map/ppermute | solution.py:288
  107.2 18.4 %collective-permute-start.22 = (f32[128,512]{1,0:T(8,128)S(1)}, f32[128,512]{1,0:T(8,128)S(1)}, u32[]{:S(2)}, u32[]{:S(2)}) collective-permute-start(f32[128,512]{1,0:T(8,128)S(1)} %constant_dynamic-update-slice_fusion.8), channel_id=1, source_target_pairs={{0,2},{1,3},{2,0},{3,1},{4,6},{5,7},{6,4},{7,5},{8,10},{9,11},{10,... | collective-permute-start | bytes 786440 | tf_op jit(solution)/shard_map/ppermute | solution.py:288
  108.7 20.9 %collective-permute-start.16 = (f32[128,512]{1,0:T(8,128)S(1)}, f32[128,512]{1,0:T(8,128)S(1)}, u32[]{:S(2)}, u32[]{:S(2)}) collective-permute-start(f32[128,512]{1,0:T(8,128)S(1)} %constant_dynamic-update-slice_fusion.14), channel_id=1, source_target_pairs={{0,2},{1,3},{2,0},{3,1},{4,6},{5,7},{6,4},{7,5},{8,10},{9,11},{10,... | collective-permute-start | bytes 786440 | tf_op jit(solution)/shard_map/ppermute | solution.py:288
  114.4 26.1 %collective-permute-start.11 = (f32[256,512]{1,0:T(8,128)S(1)}, f32[256,512]{1,0:T(8,128)S(1)}, u32[]{:S(2)}, u32[]{:S(2)}) collective-permute-start(f32[256,512]{1,0:T(8,128)S(1)} %constant_dynamic-update-slice_fusion.18), channel_id=1, source_target_pairs={{0,1},{1,0},{2,3},{3,2},{4,5},{5,4},{6,7},{7,6},{8,9},{9,8},{10,11... | collective-permute-start | bytes 1572872 | tf_op jit(solution)/shard_map/ppermute | solution.py:288
  120.0 20.5 %collective-permute-start.5 = (f32[256,512]{1,0:T(8,128)S(1)}, f32[256,512]{1,0:T(8,128)S(1)}, u32[]{:S(2)}, u32[]{:S(2)}) collective-permute-start(f32[256,512]{1,0:T(8,128)S(1)} %constant_dynamic-update-slice_fusion.24), channel_id=1, source_target_pairs={{0,1},{1,0},{2,3},{3,2},{4,5},{5,4},{6,7},{7,6},{8,9},{9,8},{10,11... | collective-permute-start | bytes 1572872 | tf_op jit(solution)/shard_map/ppermute | solution.py:288
  125.6 33.4 %collective-permute-start.23 = (f32[256,512]{1,0:T(8,128)S(1)}, f32[256,512]{1,0:T(8,128)S(1)}, u32[]{:S(2)}, u32[]{:S(2)}) collective-permute-start(f32[256,512]{1,0:T(8,128)S(1)} %constant_dynamic-update-slice_fusion.6), channel_id=1, source_target_pairs={{0,1},{1,0},{2,3},{3,2},{4,5},{5,4},{6,7},{7,6},{8,9},{9,8},{10,11... | collective-permute-start | bytes 1572872 | tf_op jit(solution)/shard_map/ppermute | solution.py:288
  129.6 29.3 %collective-permute-start.17 = (f32[256,512]{1,0:T(8,128)S(1)}, f32[256,512]{1,0:T(8,128)S(1)}, u32[]{:S(2)}, u32[]{:S(2)}) collective-permute-start(f32[256,512]{1,0:T(8,128)S(1)} %constant_dynamic-update-slice_fusion.12), channel_id=1, source_target_pairs={{0,1},{1,0},{2,3},{3,2},{4,5},{5,4},{6,7},{7,6},{8,9},{9,8},{10,11... | collective-permute-start | bytes 1572872 | tf_op jit(solution)/shard_map/ppermute | solution.py:288
  184.4 4.4 %collective-permute-start.27 = (f32[256,2048]{1,0:T(8,128)}, f32[256,2048]{1,0:T(8,128)S(1)}, u32[]{:S(2)}, u32[]{:S(2)}) collective-permute-start(f32[256,2048]{1,0:T(8,128)} %constant_dynamic-slice_fusion), channel_id=1, source_target_pairs={{0,8},{8,0},{16,24},{24,16},{1,9},{9,1},{17,25},{25,17},{2,10},{10... | collective-permute-start | bytes 6291464 | tf_op jit(solution)/shard_map/ppermute | solution.py:288
  190.6 47.7 %collective-permute-start.28 = (f32[256,2048]{1,0:T(8,128)S(1)}, f32[256,2048]{1,0:T(8,128)S(1)}, u32[]{:S(2)}, u32[]{:S(2)}) collective-permute-start(f32[256,2048]{1,0:T(8,128)S(1)} %dynamic-slice_add_fusion), channel_id=1, source_target_pairs={{0,16},{8,24},{16,0},{24,8},{1,17},{9,25},{17,1},{25,9},{2,18},{10... | collective-permute-start | bytes 6291464 | tf_op jit(solution)/shard_map/ppermute | solution.py:288
  203.8 39.6 %collective-permute-start.24 = (f32[256,512]{1,0:T(8,128)S(1)}, f32[256,512]{1,0:T(8,128)S(1)}, u32[]{:S(2)}, u32[]{:S(2)}) collective-permute-start(f32[256,512]{1,0:T(8,128)S(1)} %constant_dynamic-slice_fusion.1), channel_id=1, source_target_pairs={{0,8},{8,0},{16,24},{24,16},{1,9},{9,1},{17,25},{25,17},{2,10},{10... | collective-permute-start | bytes 1572872 | tf_op jit(solution)/shard_map/ppermute | solution.py:288
  240.9 2.5 copy-start.3
  243.4 44.8 %collective-permute-start.29 = (f32[256,2048]{1,0:T(8,128)}, f32[256,2048]{1,0:T(8,128)S(1)}, u32[]{:S(2)}, u32[]{:S(2)}) collective-permute-start(f32[256,2048]{1,0:T(8,128)} %get-tuple-element.8), channel_id=1, source_target_pairs={{0,8},{8,0},{16,24},{24,16},{1,9},{9,1},{17,25},{25,17},{2,10},{10... | collective-permute-start | bytes 6291464 | tf_op jit(solution)/shard_map/ppermute | solution.py:288
  243.5 14.4 %collective-permute-start.25 = (f32[256,512]{1,0:T(8,128)S(1)}, f32[256,512]{1,0:T(8,128)S(1)}, u32[]{:S(2)}, u32[]{:S(2)}) collective-permute-start(f32[256,512]{1,0:T(8,128)S(1)} %dynamic-slice_add_fusion.1), channel_id=1, source_target_pairs={{0,16},{8,24},{16,0},{24,8},{1,17},{9,25},{17,1},{25,9},{2,18},{10... | collective-permute-start | bytes 1572872 | tf_op jit(solution)/shard_map/ppermute | solution.py:288
  258.1 2.0 collective-permute-start.26
  260.2 1.0 copy-start.4
  297.8 8.6 %collective-permute-start.30 = (f32[512,128]{1,0:T(8,128)}, f32[512,128]{1,0:T(8,128)S(1)}, u32[]{:S(2)}, u32[]{:S(2)}) collective-permute-start(f32[512,128]{1,0:T(8,128)} %get-tuple-element.6), channel_id=1, source_target_pairs={{0,1},{1,0},{2,3},{3,2},{4,5},{5,4},{6,7},{7,6},{8,9},{9,8},{10,11... | collective-permute-start | bytes 786440 | tf_op jit(solution)/shard_map/ppermute | solution.py:288
  307.3 7.5 %collective-permute-start.31 = (f32[512,128]{1,0:T(8,128)S(1)}, f32[512,128]{1,0:T(8,128)S(1)}, u32[]{:S(2)}, u32[]{:S(2)}) collective-permute-start(f32[512,128]{1,0:T(8,128)S(1)} %add.159), channel_id=1, source_target_pairs={{0,2},{1,3},{2,0},{3,1},{4,6},{5,7},{6,4},{7,5},{8,10},{9,11},{10,... | collective-permute-start | bytes 786440 | tf_op jit(solution)/shard_map/ppermute | solution.py:288
  314.9 13.2 %collective-permute-start.32 = (f32[512,128]{1,0:T(8,128)S(1)}, f32[512,128]{1,0:T(8,128)S(1)}, u32[]{:S(2)}, u32[]{:S(2)}) collective-permute-start(f32[512,128]{1,0:T(8,128)S(1)} %add.160), channel_id=1, source_target_pairs={{0,4},{1,5},{2,6},{3,7},{4,0},{5,1},{6,2},{7,3},{8,12},{9,13},{10,... | collective-permute-start | bytes 786440 | tf_op jit(solution)/shard_map/ppermute | solution.py:288
  328.2 0.8 copy-start.5
